TPU v7x, 32 devices: a whole 2x2x4 slice. The times are simulated.
32 devices in a mesh: groups: 2 (over y), query: 16 (over z, x, core).
Axes of the slice: x: 2, y: 2, z: 4, core: 2. Of those that a mesh axis runs over, the one named last changes fastest.
Arguments:
- tokens: bfloat16 [32, 8192], P(('groups', 'query')), parts along dimension 0, may hold values from -6 to 6
- target: bfloat16 [32, 8192], P(('groups', 'query')), parts along dimension 0, may hold values from -6 to 6
- gate_weight: bfloat16 [8192, 28672], P(None, 'query'), may hold values from -0.0625 to 0.0625
- up_weight: bfloat16 [8192, 28672], P(None, 'query'), may hold values from -0.0625 to 0.0625
- down_weight: bfloat16 [28672, 8192], P('query'), may hold values from -0.03125 to 0.03125
- proj_in: bfloat16 [28672, 64], P('query'), may hold values from -0.03125 to 0.03125
- proj_out: bfloat16 [8192, 64], replicated, may hold values from -0.0625 to 0.0625
- segment_ids: int32 [32], P('groups'), parts along dimension 0, may hold values from 0 to 3, never falling along the last dimension, each value on 1 to 8 neighbouring positions
- queries: bfloat16 [1024, 4096], P('query'), may hold values from -0.09375 to 0.09375
Outputs:
- scores: float32 [1024, 8], P('query', 'groups'), parts along dimension 1
There are 2 independent parts, one for each index of `groups`. A program takes and returns all parts, laid end to end along the dimension named above; an argument that names none is the same for every part. Nothing has to cross between parts.
Inputs may be any that keep to these rules, and one draw needn't show every extreme that they name: `segment_ids`: ids never fall along the batch; each of the 4 pieces holds 1 to 8 tokens and one holds exactly 8.
All inputs are finite; a program needn't handle non-finite values.
Results may differ from a plain program's by a relative error of at most 0.0049.
Values may be sent and summed in bfloat16 or wider, within the bound.
A program may use at most 192 MiB of HBM per device.

v0:
```python
import jax
import jax.numpy as jnp
from jax import lax
from jax.sharding import PartitionSpec as P

R = 64
SEQS = 4


def local(
    tokens, target, gate_weight, up_weight, down_weight, proj_in, proj_out, segment_ids, queries
):
    token_block = lax.all_gather(tokens, "query", axis=0, tiled=True)
    gate_pre = jnp.dot(token_block, gate_weight, preferred_element_type=jnp.float32)
    up_pre = jnp.dot(token_block, up_weight, preferred_element_type=jnp.float32)
    hidden = (jax.nn.silu(gate_pre) * up_pre).astype(jnp.bfloat16)
    input_part = jnp.dot(hidden, proj_in, preferred_element_type=jnp.float32)
    out_proj = proj_out.astype(jnp.float32)
    output_own = lax.psum_scatter(
        jnp.dot(hidden, down_weight, preferred_element_type=jnp.float32),
        "query",
        scatter_dimension=0,
        tiled=True,
    )
    grad_own = output_own - target.astype(jnp.float32)
    side_own = jnp.dot(grad_own, out_proj, precision=lax.Precision.HIGHEST)
    input_side = lax.psum(input_part, "query")
    output_side = lax.all_gather(side_own, "query", axis=0, tiled=True)
    seq_index = jnp.arange(SEQS, dtype=jnp.int32)
    onehot = (segment_ids[None, :] == seq_index[:, None]).astype(jnp.float32)
    masked = onehot[:, :, None] * input_side[None, :, :]
    kronecker = jnp.einsum("sti,tj->sij", masked, output_side, precision=lax.Precision.HIGHEST)
    kronecker = kronecker.reshape(SEQS, R * R).astype(jnp.bfloat16)
    return jnp.dot(queries, kronecker.T, preferred_element_type=jnp.float32)


def solution(mesh):
    in_specs = (
        P(("groups", "query"), None),
        P(("groups", "query"), None),
        P(None, "query"),
        P(None, "query"),
        P("query", None),
        P("query", None),
        P(),
        P("groups"),
        P("query", None),
    )
    out_specs = P("query", "groups")
    return jax.shard_map(local, mesh=mesh, in_specs=in_specs, out_specs=out_specs, check_vma=False)
```

profile of v0, /device:TPU:0, one launch (start us, length us, event | category | flops | bytes accessed | tf_op | source)
XLA Modules:
  0.0 225.3 jit_solution(12422238064809729212)
XLA Ops:
  6.5 0.0 copy-start
  6.5 0.0 all-reduce.5.cloned.1.call-start
  6.5 24.9 %all-gather.1 = bf16[16,1,8192]{2,1,0:T(2,128)(2,1)S(1)} all-gather(bf16[1,1,8192]{2,1,0:T(2,128)(2,1)} %bitcast.26), channel_id=1, replica_groups=mesh['groups'=2,'query'=16] {'query'}, dimensions={0}, use_global_device_ids=true | all-gather | bytes 278528 | tf_op jit(solution)/shard_map/all_gather | solution.py:13
  31.4 11.4 %fusion.2 = f32[16,1792]{1,0:T(8,128)S(1)} fusion(bf16[8192,1792]{1,0:T(8,128)(2,1)} %param.11, bf16[16,1,8192]{2,1,0:T(2,128)(2,1)S(1)} %all-gather.1), kind=kOutput, calls=%fused_computation.6 | convolution fusion | flops 469762048 | bytes 29736960 | tf_op jit(solution)/shard_map/dot_general | solution.py:14
  42.9 0.0 copy-start.4
  42.9 0.0 copy-start.3
  42.9 0.0 copy-start.2
  42.9 0.0 copy-start.5
  42.9 0.0 copy-start.1
  43.0 11.6 %fusion = bf16[16,1792]{1,0:T(8,128)(2,1)S(1)} fusion(bf16[8192,1792]{1,0:T(8,128)(2,1)} %param.12, f32[16,1792]{1,0:T(8,128)S(1)} %fusion.2, bf16[16,1,8192]{2,1,0:T(2,128)(2,1)S(1)} %all-gather.1), kind=kOutput, calls=%fused_computation.1 | convolution fusion | flops 469934080 | bytes 29794304 | tf_op jit(solution)/shard_map/dot_general | solution.py:15
  54.5 12.2 %fusion.16 = f32[16,8192]{1,0:T(8,128)} fusion(bf16[16,1792]{1,0:T(8,128)(2,1)S(1)} %fusion, bf16[1792,8192]{1,0:T(8,128)(2,1)} %param.13), kind=kOutput, calls=%fused_computation.21 | convolution fusion | flops 469762048 | bytes 29941760 | tf_op jit(solution)/shard_map/dot_general | solution.py:20
  66.7 0.0 all-reduce.5.cloned.1.call-update
  66.7 0.0 copy-done.4
  66.8 0.0 copy-done.3
  66.8 0.7 fusion.14
  68.1 0.0 copy-done.2
  68.1 0.1 fusion.15
  68.2 86.1 %all-reduce.5.cloned.1.call-done = f32[16,8192]{1,0:T(8,128)} async-done(((f32[16,8192]{1,0:T(8,128)}), f32[16,8192]{1,0:T(8,128)}) %all-reduce.5.cloned.1.call-update) | async-done | bytes 524304
  154.3 0.0 copy-done
  154.3 0.0 copy-done.5
  154.3 2.5 %convolution_bitcast_fusion.1 = f32[64]{0:T(128)S(1)} fusion(bf16[8192,64]{0,1:T(8,128)(2,1)S(1)} %copy-done, f32[16,8192]{1,0:T(8,128)} %all-reduce.5.cloned.1.call-done, u32[]{:T(128)} %bitcast.6, bf16[1,8192]{1,0:T(2,128)(2,1)S(1)} %copy-done.5), kind=kOutput, calls=%fused_computation.4 | convolution fusion | flops 6307840 | bytes 1098496 | tf_op jit(solution)/shard_map/dot_general | solution.py:26
  156.8 0.2 dynamic-update-slice
  157.0 59.9 %all-reduce.2 = (f32[1024]{0:T(1024)S(1)}, f32[16,64]{1,0:T(8,128)S(1)}) all-reduce(f32[1024]{0:T(1024)S(1)} %dynamic-update-slice, f32[16,64]{1,0:T(8,128)S(1)} %fusion.15), channel_id=2, replica_groups=mesh['groups'=2,'query'=16] {'query'}, use_global_device_ids=true, to_apply=%add | all-reduce | flops 2048 | bytes 16384
  216.9 0.1 reshape.37
  217.0 0.5 convolution_convert_fusion
  217.5 0.1 convert_element_type.24
  217.6 0.0 copy-done.1
  217.6 0.8 convolution_bitcast_fusion
  (2 shorter events, 0.0 us)
Async XLA Ops:
  6.5 147.8 %copy-start = (bf16[8192,64]{0,1:T(8,128)(2,1)S(1)}, bf16[8192,64]{0,1:T(8,128)(2,1)}, u32[]{:S(2)}) copy-start(bf16[8192,64]{0,1:T(8,128)(2,1)} %param.15) | copy-start | bytes 3145732
  6.5 147.8 %all-reduce.5.cloned.1.call-start = ((), (), s32[]{:S(2)}) async-start(), calls=%async_computation | async-start | bytes 1048576
  42.9 23.9 %copy-start.4 = (s32[16]{0:T(128)S(1)}, s32[16]{0:T(128)}, u32[]{:S(2)}) copy-start(s32[16]{0:T(128)} %param.16) | copy-start | bytes 196
  42.9 23.9 %copy-start.3 = (u32[32]{0:T(128)S(1)}, u32[32]{0:T(128)}, u32[]{:S(2)}) copy-start(u32[32]{0:T(128)} %constant.7) | copy-start | bytes 388
  42.9 25.2 %copy-start.2 = (bf16[1792,64]{0,1:T(8,128)(2,1)S(1)}, bf16[1792,64]{0,1:T(8,128)(2,1)}, u32[]{:S(2)}) copy-start(bf16[1792,64]{0,1:T(8,128)(2,1)} %param.14) | copy-start | bytes 688132
  42.9 111.4 %copy-start.5 = (bf16[1,8192]{1,0:T(2,128)(2,1)S(1)}, bf16[1,8192]{1,0:T(2,128)(2,1)}, u32[]{:S(2)}) copy-start(bf16[1,8192]{1,0:T(2,128)(2,1)} %param.10) | copy-start | bytes 49156
  42.9 174.7 %copy-start.1 = (bf16[64,4096]{1,0:T(8,128)(2,1)S(1)}, bf16[64,4096]{1,0:T(8,128)(2,1)}, u32[]{:S(2)}) copy-start(bf16[64,4096]{1,0:T(8,128)(2,1)} %param.17) | copy-start | bytes 1572868
Sparse Core Ops, SparseCore 0:
  66.9 87.3 all-reduce.4
where the time goes:
time: 225 us
  waiting for transfers between devices  86.1 us (38%)
  blocking collectives  84.8 us (38%)
  matrix products  39.1 us (17%)
  between operations  14.1 us (6%)
    unnamed x2, waiting for transfers between devices  86.1 us
    unnamed x1, blocking collectives  59.9 us
    all_gather x1, blocking collectives, local(): token_block = lax.all_gather(tokens, 'query', axis=0, tiled=True)  24.9 us
    dot_general x1, matrix products, local(): jnp.dot(hidden, down_weight, preferred_element_type=jnp.float32)  12.2 us
    dot_general x1, matrix products, local(): up_pre = jnp.dot(token_block, up_weight, preferred_element_type=jnp.float32)  11.6 us
    dot_general x1, matrix products, local(): jnp.dot(token_block, gate_weight, preferred_element_type=jnp.float32)  11.4 us
  transfers between devices with their start and end apart: 1, of which 1 were waited for; matrix products, arithmetic and copies ran while one was open for 0% of the time, Pallas kernels for 0%

commit v1 on v0

v1 whole, which is shorter than its diff:
```python
import functools

import jax
import jax.numpy as jnp
from jax import lax
from jax.experimental import pallas as pl
from jax.experimental.pallas import tpu as pltpu
from jax.sharding import PartitionSpec as P

SEQS = 4
DEPTH = 512
SLOTS = 5
F32 = jnp.float32
BF16 = jnp.bfloat16
MESH = pl.DeviceIdType.MESH


def rows_per_chunk(total, most):
    return max(size for size in range(16, most + 1, 16) if total % size == 0)


def split(value):
    high = value.astype(BF16)
    return high, (value - high.astype(F32)).astype(BF16)


def kernel(
    n, tokens, target, gate, up, down, proj_in, proj_out, segment_ids, queries, scores,
    gate_ring, up_ring, down_buf, pin, pout, tgt, qbuf, gathered, x32, x16, expand, mixed,
    gate_acc, up_acc, payload, parts,
    gate_sem, up_sem, down_sem, load_sem, tok_send, tok_recv, part_send, part_recv,
):
    me = lax.axis_index("query")
    width, hidden_units = gate.shape
    rank = proj_in.shape[1]
    count = x16.shape[0]
    down_rows = down_buf.shape[1]
    down_chunks = down_buf.shape[0]
    steps = width // DEPTH
    slots = gate_ring.shape[0]

    def peer(d):
        return lax.rem(me + d, n)

    barrier = pltpu.get_barrier_semaphore()

    @pl.loop(1, n)
    def _(d):
        pl.semaphore_signal(barrier, inc=1, device_id={"query": peer(d)}, device_id_type=MESH)

    loads = [
        pltpu.make_async_copy(src, dst, load_sem.at[i])
        for i, (src, dst) in enumerate(
            [
                (proj_out, pout),
                (tokens, gathered.at[me]),
                (target, tgt),
                (proj_in, pin),
                (queries, qbuf),
            ]
        )
    ]

    def down_copy(c):
        at = pl.ds(pl.multiple_of(c * down_rows, down_rows), down_rows)
        return pltpu.make_async_copy(down.at[at, :], down_buf.at[c], down_sem.at[c])

    def ring_copies(c, slot):
        at = pl.ds(pl.multiple_of(c * DEPTH, DEPTH), DEPTH)
        return (
            pltpu.make_async_copy(gate.at[at, :], gate_ring.at[slot], gate_sem.at[slot]),
            pltpu.make_async_copy(up.at[at, :], up_ring.at[slot], up_sem.at[slot]),
        )

    for load in loads[:4]:
        load.start()
    for c in range(down_chunks):
        down_copy(c).start()
    for c in range(slots):
        for copy in ring_copies(c, c):
            copy.start()

    pl.semaphore_wait(barrier, n - 1)

    def token_copy(d):
        return pltpu.make_async_remote_copy(
            src_ref=tokens,
            dst_ref=gathered.at[me],
            send_sem=tok_send.at[d],
            recv_sem=tok_recv.at[me],
            device_id={"query": peer(d)},
            device_id_type=MESH,
        )

    @pl.loop(1, n)
    def _(d):
        token_copy(d).start()

    owner = lax.broadcasted_iota(jnp.int32, expand.shape, 1) // rank
    expand[...] = jnp.where(
        lax.broadcasted_iota(jnp.int32, expand.shape, 0) == owner, 1.0, 0.0
    ).astype(BF16)
    gate_acc[...] = jnp.zeros_like(gate_acc)
    up_acc[...] = jnp.zeros_like(up_acc)

    for load in loads[:4]:
        load.wait()
    target_side = jnp.dot(tgt[...], pout[...], preferred_element_type=F32)

    @pl.loop(0, down_chunks)
    def _(c):
        down_copy(c).wait()
        side = jnp.dot(down_buf[c], pout[...], preferred_element_type=F32)
        at = pl.ds(pl.multiple_of(c * down_rows, down_rows), down_rows)
        high, low = split(jnp.concatenate([pin[at, :].astype(F32), side], axis=1))
        mixed[at, : 2 * rank] = high
        mixed[at, 2 * rank :] = low

    @pl.loop(1, n)
    def _(d):
        source = peer(d)
        pltpu.make_async_remote_copy(
            src_ref=tokens,
            dst_ref=gathered.at[source],
            send_sem=tok_send.at[d],
            recv_sem=tok_recv.at[source],
            device_id={"query": source},
            device_id_type=MESH,
        ).wait_recv()

    @pl.loop(0, n)
    def _(t):
        x32[pl.ds(t, 1), :] = gathered[t].astype(F32)

    x16[...] = x32[...].astype(BF16)
    loads[4].start()

    @pl.loop(0, steps)
    def _(c):
        slot = lax.rem(c, slots)
        for copy in ring_copies(c, slot):
            copy.wait()
        x = x16[:, pl.ds(pl.multiple_of(c * DEPTH, DEPTH), DEPTH)]
        gate_acc[...] += jnp.dot(x, gate_ring[slot], preferred_element_type=F32)
        up_acc[...] += jnp.dot(x, up_ring[slot], preferred_element_type=F32)

        @pl.when(c + slots < steps)
        def _():
            for copy in ring_copies(c + slots, slot):
                copy.start()

    gate_pre = gate_acc[...]
    hidden = (gate_pre / (1.0 + jnp.exp(-gate_pre)) * up_acc[...]).astype(BF16)
    sides = jnp.dot(hidden, mixed[...], preferred_element_type=F32)
    sides = sides[:, : 2 * rank] + sides[:, 2 * rank :]
    shifted = jnp.concatenate([jnp.zeros_like(target_side), target_side], axis=1)
    own_row = lax.broadcasted_iota(jnp.int32, sides.shape, 0) == me
    sides = sides - jnp.where(own_row, jnp.broadcast_to(shifted, sides.shape), 0.0)
    payload[...] = sides.astype(payload.dtype)

    def part_copy(d, slot):
        return pltpu.make_async_remote_copy(
            src_ref=payload,
            dst_ref=parts.at[slot],
            send_sem=part_send.at[d],
            recv_sem=part_recv.at[slot],
            device_id={"query": peer(d)},
            device_id_type=MESH,
        )

    @pl.loop(1, n)
    def _(d):
        part_copy(d, me).start()

    parts[me] = payload[...]
    loads[4].wait()
    marks = (
        lax.broadcasted_iota(jnp.int32, (2 * SEQS, count), 0) == segment_ids[...]
    ).astype(BF16)

    @pl.loop(1, n)
    def _(d):
        part_copy(d, peer(d)).wait_recv()

    total = lax.fori_loop(
        0, n, lambda p, t: t + parts[p].astype(F32), jnp.zeros(payload.shape, F32)
    )
    high, low = split(total)
    spread = jnp.dot(
        jnp.concatenate([high, low], axis=0), expand[...], preferred_element_type=F32
    )
    spread = spread[:count] + spread[count:]
    output_side = total[:, rank:]
    doubled = jnp.concatenate([output_side, output_side], axis=1)
    pairs = spread * jnp.concatenate([doubled] * (rank // 2), axis=1)
    high, low = split(pairs)
    kronecker = jnp.dot(marks, high, preferred_element_type=F32) + jnp.dot(
        marks, low, preferred_element_type=F32
    )
    result = lax.dot_general(
        qbuf[...],
        kronecker.astype(BF16),
        (((1,), (1,)), ((), ())),
        preferred_element_type=F32,
    )
    scores[...] = result[:, :SEQS]

    @pl.loop(1, n)
    def _(d):
        token_copy(d).wait_send()
        part_copy(d, me).wait_send()


def solution(mesh):
    n = mesh.shape["query"]

    def local(tokens, target, gate, up, down, proj_in, proj_out, segment_ids, queries):
        width, units = gate.shape
        rank = proj_in.shape[1]
        count = segment_ids.shape[0]
        down_rows = rows_per_chunk(units, 256)
        down_chunks = units // down_rows
        any_spec = pl.BlockSpec(memory_space=pl.ANY)
        vmem_spec = pl.BlockSpec(memory_space=pltpu.VMEM)
        dma = pltpu.SemaphoreType.DMA
        return pl.pallas_call(
            functools.partial(kernel, n),
            out_shape=jax.ShapeDtypeStruct((queries.shape[0], SEQS), F32),
            in_specs=[any_spec] * 7 + [vmem_spec, any_spec],
            out_specs=vmem_spec,
            scratch_shapes=[
                pltpu.VMEM((SLOTS, DEPTH, units), BF16),
                pltpu.VMEM((SLOTS, DEPTH, units), BF16),
                pltpu.VMEM((down_chunks, down_rows, width), BF16),
                pltpu.VMEM((units, rank), BF16),
                pltpu.VMEM((width, rank), BF16),
                pltpu.VMEM((1, width), BF16),
                pltpu.VMEM(queries.shape, BF16),
                pltpu.VMEM((n, 1, width), BF16),
                pltpu.VMEM((count, width), F32),
                pltpu.VMEM((count, width), BF16),
                pltpu.VMEM((2 * rank, rank * rank), BF16),
                pltpu.VMEM((units, 4 * rank), BF16),
                pltpu.VMEM((count, units), F32),
                pltpu.VMEM((count, units), F32),
                pltpu.VMEM((count, 2 * rank), F32),
                pltpu.VMEM((n, count, 2 * rank), F32),
                dma((SLOTS,)),
                dma((SLOTS,)),
                dma((down_chunks,)),
                dma((5,)),
                dma((n,)),
                dma((n,)),
                dma((n,)),
                dma((n,)),
            ],
            compiler_params=pltpu.CompilerParams(
                collective_id=0, has_side_effects=True, vmem_limit_bytes=63 * 1024 * 1024
            ),
            name="forget",
        )(
            tokens, target, gate, up, down, proj_in, proj_out,
            segment_ids.reshape(1, count), queries,
        )

    in_specs = (
        P(("groups", "query"), None),
        P(("groups", "query"), None),
        P(None, "query"),
        P(None, "query"),
        P("query", None),
        P("query", None),
        P(),
        P("groups"),
        P("query", None),
    )
    return jax.shard_map(
        local, mesh=mesh, in_specs=in_specs, out_specs=P("query", "groups"), check_vma=False
    )
```

time: 225 us -> 54.3 us (0.24)
  waiting for transfers between devices: 86.1 us -> 0 us
  blocking collectives: 84.8 us -> 0 us
  Pallas kernels: 0 us -> 48 us
  matrix products: 39.1 us -> 0 us
  between operations: 14.1 us -> 0.01 us
  local copies, waits for them, and re-layouts: 1.07 us -> 6.1 us
    unnamed x2 -> x0, waiting for transfers between devices: 86.1 us -> none
    unnamed x1 -> x0, blocking collectives: 59.9 us -> none
    pallas_call x0 -> x1, Pallas kernels: none -> 48 us  [local(): pl.pallas_call(functools.partial(kernel, n), out_shape=jax.ShapeDtypeStru...]
    dot_general x7 -> x0, matrix products: 39.1 us -> none  [the longest x1 12.2 us: local(): jnp.dot(hidden, down_weight, preferred_element_type=jnp.float32)]
    all_gather x1 -> x0, blocking collectives: 24.9 us -> none  [local(): token_block = lax.all_gather(tokens, 'query', axis=0, tiled=True)]
    unnamed x15 -> x2, local copies, waits for them, and re-layouts: 0.89 us -> 4.69 us
  transfers between devices with their start and end apart: 1 -> 0, of which waited for: 1 -> 0; matrix products, arithmetic and copies ran while one was open for 0% -> 0% of each run, Pallas kernels for 0% -> 0%
where the time goes in v1:
time: 54.3 us; the launch traced here: 54.1 us
  Pallas kernels  48 us (88%)
  local copies, waits for them, and re-layouts  6.1 us (11%)
    pallas_call x1, Pallas kernels, local(): pl.pallas_call(functools.partial(kernel, n), out_shape=jax.ShapeDtypeStru...  48 us
    unnamed x2, local copies, waits for them, and re-layouts  4.69 us
    pallas_call x1, local copies, waits for them, and re-layouts, local(): pl.pallas_call(functools.partial(kernel, n), out_shape=jax.ShapeDtypeStru...  1.41 us

profile of v1, /device:TPU:0, one launch (start us, length us, event | category | flops | bytes accessed | tf_op | source)
XLA Modules:
  0.0 54.1 jit_solution(6514388116905745631)
XLA Ops:
  0.0 1.9 %copy.10.proj_in = bf16[1792,64]{1,0:T(8,128)(2,1)} copy(bf16[1792,64]{0,1:T(8,128)(2,1)} %param.14) | data formatting | bytes 458752 | tf_op args[5]
  1.9 2.8 %copy.11.proj_out = bf16[8192,64]{1,0:T(8,128)(2,1)} copy(bf16[8192,64]{0,1:T(8,128)(2,1)} %param.15) | data formatting | bytes 2097152 | tf_op args[6]
  4.7 48.0 %forget.1 = f32[64,4]{1,0:T(8,128)} custom-call(bf16[1,8192]{1,0:T(2,128)(2,1)} %tokens.1, bf16[1,8192]{1,0:T(2,128)(2,1)} %target.1, bf16[8192,1792]{1,0:T(8,128)(2,1)} %gate.1, bf16[8192,1792]{1,0:T(8,128)(2,1)} %up.1, bf16[1792,8192]{1,0:T(8,128)(2,1)} %down.1, bf16[1792,64]{1,0:T(8,128)(2,1)} %copy.10.proj_in, bf16[8192,64]{1,0:T(8,128)(2,1)} %copy.11.proj_out, ...), custom_call_target="tpu_custom_call" | custom-call | tf_op jit(solution)/shard_map/forget/pallas_call | solution.py:226
  52.7 1.4 %copy.12 = f32[64,4]{0,1:T(4,128)} copy(f32[64,4]{1,0:T(8,128)} %forget.1) | data formatting | bytes 2048 | tf_op jit(solution)/shard_map/forget/pallas_call | solution.py:226

commit v2 on v1

v2 whole, which is shorter than its diff:
```python
import functools

import jax
import jax.numpy as jnp
from jax import lax
from jax.experimental import pallas as pl
from jax.experimental.pallas import tpu as pltpu
from jax.sharding import PartitionSpec as P

SEQS = 4
DEPTH = 512
SLOTS = 10
DOWN_SLOTS = 8
LANES = 128
F32 = jnp.float32
BF16 = jnp.bfloat16
MESH = pl.DeviceIdType.MESH


def split(value):
    high = value.astype(BF16)
    return high, (value - high.astype(F32)).astype(BF16)


def dot(a, b):
    return jnp.dot(a, b, preferred_element_type=F32)


def dot_lanes(a, b):
    return lax.dot_general(a, b, (((1,), (1,)), ((), ())), preferred_element_type=F32)


def pack(value):
    half = value.shape[0] // 2
    return jnp.concatenate([value[:half], value[half:]], axis=1)


def kernel(
    n, tokens, target, gate, up, down, proj_in, proj_out, segment_ids, queries, scores,
    gate_ring, up_ring, down_ring, pin, pout, tok, tgt, qbuf, slab32, slab, gathered, x32, x16,
    expand, spread, gate_acc, up_acc, hidden_ref, side_acc, payload_a, payload_b, parts_a, parts_b,
    gate_sem, up_sem, down_sem, load_sem, tok_send, tok_recv, a_send, a_recv, b_send, b_recv,
):
    me = lax.axis_index("query")
    width = gate.shape[0]
    rank = proj_in.shape[0]
    count = x16.shape[0]
    pieces = width // LANES
    steps = width // DEPTH
    slots = gate_ring.shape[0]
    down_slots = down_ring.shape[0]

    def peer(d):
        return lax.rem(me + d, n)

    barrier = pltpu.get_barrier_semaphore()

    @pl.loop(1, n)
    def _(d):
        pl.semaphore_signal(barrier, inc=1, device_id={"query": peer(d)}, device_id_type=MESH)

    loads = [
        pltpu.make_async_copy(src, dst, load_sem.at[i])
        for i, (src, dst) in enumerate(
            [(tokens, tok), (target, tgt), (proj_out, pout), (proj_in, pin), (queries, qbuf)]
        )
    ]

    def chunk(c):
        return pl.ds(pl.multiple_of(c * DEPTH, DEPTH), DEPTH)

    def ring_copies(c, slot):
        return (
            pltpu.make_async_copy(gate.at[chunk(c), :], gate_ring.at[slot], gate_sem.at[slot]),
            pltpu.make_async_copy(up.at[chunk(c), :], up_ring.at[slot], up_sem.at[slot]),
        )

    def down_copy(c):
        slot = lax.rem(c, down_slots)
        return pltpu.make_async_copy(down.at[:, chunk(c)], down_ring.at[slot], down_sem.at[slot])

    for load in loads[:3]:
        load.start()
    for c in range(slots):
        for copy in ring_copies(c, c):
            copy.start()
    loads[3].start()
    loads[4].start()

    loads[0].wait()
    for k in range(pieces):
        slab32[k : k + 1, :] = tok[:, k * LANES : (k + 1) * LANES].astype(F32)
    slab[...] = slab32[...].astype(BF16)
    gathered[me] = slab[...]

    pl.semaphore_wait(barrier, n - 1)

    def push(src, dst, send, recv, d, slot):
        return pltpu.make_async_remote_copy(
            src_ref=src,
            dst_ref=dst.at[slot],
            send_sem=send.at[d],
            recv_sem=recv.at[slot],
            device_id={"query": peer(d)},
            device_id_type=MESH,
        )

    token_push = functools.partial(push, slab, gathered, tok_send, tok_recv)
    a_push = functools.partial(push, payload_a, parts_a, a_send, a_recv)
    b_push = functools.partial(push, payload_b, parts_b, b_send, b_recv)

    def start_all(copy):
        @pl.loop(1, n)
        def _(d):
            copy(d, me).start()

    def receive_all(copy):
        @pl.loop(1, n)
        def _(d):
            copy(d, peer(d)).wait_recv()

    start_all(token_push)

    owner = lax.broadcasted_iota(jnp.int32, expand.shape, 1) // rank
    expand[...] = jnp.where(
        lax.broadcasted_iota(jnp.int32, expand.shape, 0) == owner, 1.0, 0.0
    ).astype(BF16)
    gate_acc[...] = jnp.zeros_like(gate_acc)
    up_acc[...] = jnp.zeros_like(up_acc)
    side_acc[...] = jnp.zeros_like(side_acc)
    loads[1].wait()
    loads[2].wait()
    target_side = dot_lanes(tgt[...], pout[...])

    receive_all(token_push)
    x32[...] = gathered[...].reshape(n * pieces, LANES).astype(F32)
    for k in range(pieces):
        x16[:, k * LANES : (k + 1) * LANES] = x32[pl.ds(k, n, stride=pieces), :].astype(BF16)

    @pl.loop(0, steps)
    def _(c):
        slot = lax.rem(c, slots)
        for copy in ring_copies(c, slot):
            copy.wait()
        x = x16[:, chunk(c)]
        gate_acc[...] += dot(x, gate_ring[slot])
        up_acc[...] += dot(x, up_ring[slot])

        @pl.when(c + slots < steps)
        def _():
            for copy in ring_copies(c + slots, slot):
                copy.start()

        @pl.when(c < down_slots)
        def _():
            down_copy(c).start()

    gate_pre = gate_acc[...]
    hidden = (gate_pre / (1.0 + jnp.exp(-gate_pre)) * up_acc[...]).astype(BF16)
    hidden_ref[...] = hidden
    loads[3].wait()
    payload_a[...] = pack(dot_lanes(hidden, pin[...]))
    start_all(a_push)
    parts_a[me] = payload_a[...]

    def down_step(c):
        down_copy(c).wait()
        high, low = split(dot(hidden_ref[...], down_ring[lax.rem(c, down_slots)]))
        side_acc[...] += dot_lanes(jnp.concatenate([high, low], axis=0), pout[:, chunk(c)])

        @pl.when(c + down_slots < steps)
        def _():
            down_copy(c + down_slots).start()

    def sum_parts(parts):
        return lax.fori_loop(
            0, n, lambda p, t: t + parts[p], jnp.zeros(parts.shape[1:], F32)
        )

    pl.loop(0, steps // 2)(down_step)

    receive_all(a_push)
    total = sum_parts(parts_a)
    input_side = jnp.concatenate([total[:, :rank], total[:, rank:]], axis=0)
    high, low = split(input_side)
    wide = dot(jnp.concatenate([high, low], axis=0), expand[...])
    spread[...] = wide[:count] + wide[count:]
    loads[4].wait()

    pl.loop(steps // 2, steps)(down_step)

    side = side_acc[:count, :] + side_acc[count:, :]
    own_row = lax.broadcasted_iota(jnp.int32, side.shape, 0) == me
    side = side - jnp.where(own_row, jnp.broadcast_to(target_side, side.shape), 0.0)
    payload_b[...] = pack(side)
    start_all(b_push)
    parts_b[me] = payload_b[...]
    marks = (
        lax.broadcasted_iota(jnp.int32, (2 * SEQS, count), 0) == segment_ids[...]
    ).astype(BF16)

    receive_all(b_push)
    total = sum_parts(parts_b)
    first, second = total[:, :rank], total[:, rank:]
    doubled = jnp.concatenate(
        [jnp.concatenate([first, first], axis=1), jnp.concatenate([second, second], axis=1)],
        axis=0,
    )
    pairs = spread[...] * jnp.concatenate([doubled] * (rank // 2), axis=1)
    high, low = split(pairs)
    kronecker = dot(marks, high) + dot(marks, low)
    scores[...] = dot_lanes(kronecker.astype(BF16), qbuf[...])[:SEQS]

    @pl.loop(1, n)
    def _(d):
        token_push(d, me).wait_send()
        a_push(d, me).wait_send()
        b_push(d, me).wait_send()


def solution(mesh):
    n = mesh.shape["query"]

    def local(tokens, target, gate, up, down, proj_in, proj_out, segment_ids, queries):
        width, units = gate.shape
        rank = proj_in.shape[1]
        count = segment_ids.shape[0]
        pieces = width // LANES
        any_spec = pl.BlockSpec(memory_space=pl.ANY)
        vmem_spec = pl.BlockSpec(memory_space=pltpu.VMEM)
        dma = pltpu.SemaphoreType.DMA
        return pl.pallas_call(
            functools.partial(kernel, n),
            out_shape=jax.ShapeDtypeStruct((SEQS, queries.shape[0]), F32),
            in_specs=[any_spec] * 7 + [vmem_spec, any_spec],
            out_specs=vmem_spec,
            scratch_shapes=[
                pltpu.VMEM((SLOTS, DEPTH, units), BF16),
                pltpu.VMEM((SLOTS, DEPTH, units), BF16),
                pltpu.VMEM((DOWN_SLOTS, units, DEPTH), BF16),
                pltpu.VMEM((rank, units), BF16),
                pltpu.VMEM((rank, width), BF16),
                pltpu.VMEM((1, width), BF16),
                pltpu.VMEM((1, width), BF16),
                pltpu.VMEM(queries.shape, BF16),
                pltpu.VMEM((pieces, LANES), F32),
                pltpu.VMEM((pieces, LANES), BF16),
                pltpu.VMEM((n, pieces, LANES), BF16),
                pltpu.VMEM((n * pieces, LANES), F32),
                pltpu.VMEM((count, width), BF16),
                pltpu.VMEM((rank, rank * rank), BF16),
                pltpu.VMEM((count, rank * rank), F32),
                pltpu.VMEM((count, units), F32),
                pltpu.VMEM((count, units), F32),
                pltpu.VMEM((count, units), BF16),
                pltpu.VMEM((2 * count, rank), F32),
                pltpu.VMEM((count // 2, 2 * rank), F32),
                pltpu.VMEM((count // 2, 2 * rank), F32),
                pltpu.VMEM((n, count // 2, 2 * rank), F32),
                pltpu.VMEM((n, count // 2, 2 * rank), F32),
                dma((SLOTS,)),
                dma((SLOTS,)),
                dma((DOWN_SLOTS,)),
                dma((5,)),
                dma((n,)),
                dma((n,)),
                dma((n,)),
                dma((n,)),
                dma((n,)),
                dma((n,)),
            ],
            compiler_params=pltpu.CompilerParams(
                collective_id=0, has_side_effects=True, vmem_limit_bytes=63 * 1024 * 1024
            ),
            name="forget",
        )(
            tokens, target, gate, up, down, proj_in.T, proj_out.T,
            segment_ids.reshape(1, count), queries,
        ).T

    in_specs = (
        P(("groups", "query"), None),
        P(("groups", "query"), None),
        P(None, "query"),
        P(None, "query"),
        P("query", None),
        P("query", None),
        P(),
        P("groups"),
        P("query", None),
    )
    return jax.shard_map(
        local, mesh=mesh, in_specs=in_specs, out_specs=P("query", "groups"), check_vma=False
    )
```

time: 54.3 us -> 45.6 us (0.84)
  local copies, waits for them, and re-layouts: 6.1 us -> 1.26 us
  Pallas kernels: 48 us -> 44.2 us
    pallas_call x1, Pallas kernels: 48 us -> 44.2 us  [local(): pl.pallas_call(functools.partial(kernel, n), out_shape=jax.ShapeDtypeStru...]
    unnamed x2 -> x1, local copies, waits for them, and re-layouts: 4.69 us -> 1.26 us
    pallas_call x1 -> x0, local copies, waits for them, and re-layouts: 1.41 us -> none  [local(): pl.pallas_call(functools.partial(kernel, n), out_shape=jax.ShapeDtypeStru...]
where the time goes in v2:
time: 45.6 us; the launch traced here: 45.4 us
  Pallas kernels  44.2 us (97%)
  local copies, waits for them, and re-layouts  1.26 us (3%)
    pallas_call x1, Pallas kernels, local(): pl.pallas_call(functools.partial(kernel, n), out_shape=jax.ShapeDtypeStru...  44.2 us
    unnamed x1, local copies, waits for them, and re-layouts  1.26 us

profile of v2, /device:TPU:0, one launch (start us, length us, event | category | flops | bytes accessed | tf_op | source)
XLA Modules:
  0.0 45.4 jit_solution(2113085215253993178)
XLA Ops:
  0.0 44.2 %forget.1 = f32[4,64]{1,0:T(4,128)} custom-call(bf16[1,8192]{1,0:T(2,128)(2,1)} %tokens.1, bf16[1,8192]{1,0:T(2,128)(2,1)} %target.1, bf16[8192,1792]{1,0:T(8,128)(2,1)} %gate.1, bf16[8192,1792]{1,0:T(8,128)(2,1)} %up.1, bf16[1792,8192]{1,0:T(8,128)(2,1)} %down.1, bf16[64,1792]{1,0:T(8,128)(2,1)} %bitcast.5, bf16[64,8192]{1,0:T(8,128)(2,1)} %bitcast.4, ...), custom_call_target="tpu_custom_call" | custom-call | tf_op jit(solution)/shard_map/forget/pallas_call | solution.py:232
  44.2 1.3 %copy.11 = f32[64,4]{0,1:T(4,128)} copy(f32[64,4]{0,1:T(4,128)} %bitcast.6) | data formatting | bytes 2048

commit v3 on v2

--- a/solution.py
+++ b/solution.py
@@ -8,9 +8,9 @@
 from jax.sharding import PartitionSpec as P
 
 SEQS = 4
-DEPTH = 512
-SLOTS = 10
-DOWN_SLOTS = 8
+DEPTH = 1024
+SLOTS = 5
+DOWN_SLOTS = 4
 LANES = 128
 F32 = jnp.float32
 BF16 = jnp.bfloat16
@@ -38,7 +38,7 @@
 def kernel(
     n, tokens, target, gate, up, down, proj_in, proj_out, segment_ids, queries, scores,
     gate_ring, up_ring, down_ring, pin, pout, tok, tgt, qbuf, slab32, slab, gathered, x32, x16,
-    expand, spread, gate_acc, up_acc, hidden_ref, side_acc, payload_a, payload_b, parts_a, parts_b,
+    expand, spread, gate_acc, up_acc, hidden_ref, block, side_acc, payload_a, payload_b, parts_a, parts_b,
     gate_sem, up_sem, down_sem, load_sem, tok_send, tok_recv, a_send, a_recv, b_send, b_recv,
 ):
     me = lax.axis_index("query")
@@ -163,31 +163,35 @@
     start_all(a_push)
     parts_a[me] = payload_a[...]
 
-    def down_step(c):
+    def down_dot(c):
         down_copy(c).wait()
         high, low = split(dot(hidden_ref[...], down_ring[lax.rem(c, down_slots)]))
-        side_acc[...] += dot_lanes(jnp.concatenate([high, low], axis=0), pout[:, chunk(c)])
-
+        return jnp.concatenate([high, low], axis=0)
+
+    def project(c):
+        side_acc[...] += dot_lanes(block[...], pout[:, chunk(c)])
+
+    def refill(c):
         @pl.when(c + down_slots < steps)
         def _():
             down_copy(c + down_slots).start()
 
+    block[...] = down_dot(0)
+    refill(0)
+
+    @pl.loop(1, steps)
+    def _(c):
+        new = down_dot(c)
+        project(c - 1)
+        block[...] = new
+        refill(c)
+
+    project(steps - 1)
+
     def sum_parts(parts):
         return lax.fori_loop(
-            0, n, lambda p, t: t + parts[p], jnp.zeros(parts.shape[1:], F32)
+            0, n, lambda p, t: t + parts[p], jnp.zeros(parts.shape[1:], F32), unroll=8
         )
-
-    pl.loop(0, steps // 2)(down_step)
-
-    receive_all(a_push)
-    total = sum_parts(parts_a)
-    input_side = jnp.concatenate([total[:, :rank], total[:, rank:]], axis=0)
-    high, low = split(input_side)
-    wide = dot(jnp.concatenate([high, low], axis=0), expand[...])
-    spread[...] = wide[:count] + wide[count:]
-    loads[4].wait()
-
-    pl.loop(steps // 2, steps)(down_step)
 
     side = side_acc[:count, :] + side_acc[count:, :]
     own_row = lax.broadcasted_iota(jnp.int32, side.shape, 0) == me
@@ -198,6 +202,14 @@
     marks = (
         lax.broadcasted_iota(jnp.int32, (2 * SEQS, count), 0) == segment_ids[...]
     ).astype(BF16)
+
+    receive_all(a_push)
+    total = sum_parts(parts_a)
+    input_side = jnp.concatenate([total[:, :rank], total[:, rank:]], axis=0)
+    high, low = split(input_side)
+    wide = dot(jnp.concatenate([high, low], axis=0), expand[...])
+    spread[...] = wide[:count] + wide[count:]
+    loads[4].wait()
 
     receive_all(b_push)
     total = sum_parts(parts_b)
@@ -253,6 +265,7 @@
                 pltpu.VMEM((count, units), F32),
                 pltpu.VMEM((count, units), F32),
                 pltpu.VMEM((count, units), BF16),
+                pltpu.VMEM((2 * count, DEPTH), BF16),
                 pltpu.VMEM((2 * count, rank), F32),
                 pltpu.VMEM((count // 2, 2 * rank), F32),
                 pltpu.VMEM((count // 2, 2 * rank), F32),

time: 45.6 us -> 42 us (0.921)
  Pallas kernels: 44.2 us -> 40.6 us
    pallas_call x1, Pallas kernels: 44.2 us -> 40.6 us  [local(): pl.pallas_call(functools.partial(kernel, n), out_shape=jax.ShapeDtypeStru...]
where the time goes in v3:
time: 42 us; the launch traced here: 41.8 us
  Pallas kernels  40.6 us (97%)
  local copies, waits for them, and re-layouts  1.26 us (3%)
    pallas_call x1, Pallas kernels, local(): pl.pallas_call(functools.partial(kernel, n), out_shape=jax.ShapeDtypeStru...  40.6 us
    unnamed x1, local copies, waits for them, and re-layouts  1.26 us

profile of v3, /device:TPU:0, one launch (start us, length us, event | category | flops | bytes accessed | tf_op | source)
XLA Modules:
  0.0 41.8 jit_solution(14587382729094919427)
XLA Ops:
  0.0 40.6 %forget.1 = f32[4,64]{1,0:T(4,128)} custom-call(bf16[1,8192]{1,0:T(2,128)(2,1)} %tokens.1, bf16[1,8192]{1,0:T(2,128)(2,1)} %target.1, bf16[8192,1792]{1,0:T(8,128)(2,1)} %gate.1, bf16[8192,1792]{1,0:T(8,128)(2,1)} %up.1, bf16[1792,8192]{1,0:T(8,128)(2,1)} %down.1, bf16[64,1792]{1,0:T(8,128)(2,1)} %bitcast.5, bf16[64,8192]{1,0:T(8,128)(2,1)} %bitcast.4, ...), custom_call_target="tpu_custom_call" | custom-call | tf_op jit(solution)/shard_map/forget/pallas_call | solution.py:244
  40.6 1.3 %copy.11 = f32[64,4]{0,1:T(4,128)} copy(f32[64,4]{0,1:T(4,128)} %bitcast.6) | data formatting | bytes 2048

commit v4 on v3

--- a/solution.py
+++ b/solution.py
@@ -199,8 +199,9 @@
     payload_b[...] = pack(side)
     start_all(b_push)
     parts_b[me] = payload_b[...]
+    segments = jnp.concatenate([segment_ids[...], segment_ids[...]], axis=1)
     marks = (
-        lax.broadcasted_iota(jnp.int32, (2 * SEQS, count), 0) == segment_ids[...]
+        lax.broadcasted_iota(jnp.int32, (2 * SEQS, 2 * count), 0) == segments
     ).astype(BF16)
 
     receive_all(a_push)
@@ -210,6 +211,12 @@
     wide = dot(jnp.concatenate([high, low], axis=0), expand[...])
     spread[...] = wide[:count] + wide[count:]
     loads[4].wait()
+
+    @pl.loop(1, n)
+    def _(d):
+        token_push(d, me).wait_send()
+        a_push(d, me).wait_send()
+        b_push(d, me).wait_send()
 
     receive_all(b_push)
     total = sum_parts(parts_b)
@@ -220,14 +227,8 @@
     )
     pairs = spread[...] * jnp.concatenate([doubled] * (rank // 2), axis=1)
     high, low = split(pairs)
-    kronecker = dot(marks, high) + dot(marks, low)
+    kronecker = dot(marks, jnp.concatenate([high, low], axis=0))
     scores[...] = dot_lanes(kronecker.astype(BF16), qbuf[...])[:SEQS]
-
-    @pl.loop(1, n)
-    def _(d):
-        token_push(d, me).wait_send()
-        a_push(d, me).wait_send()
-        b_push(d, me).wait_send()
 
 
 def solution(mesh):

time: 42 us -> 41.8 us (level)
  no operation moved by 1% of the time
where the time goes in v4:
time: 41.8 us; the launch traced here: 41.7 us
  Pallas kernels  40.4 us (97%)
  local copies, waits for them, and re-layouts  1.26 us (3%)
    pallas_call x1, Pallas kernels, local(): pl.pallas_call(functools.partial(kernel, n), out_shape=jax.ShapeDtypeStru...  40.4 us
    unnamed x1, local copies, waits for them, and re-layouts  1.26 us

profile of v4, /device:TPU:0, one launch (start us, length us, event | category | flops | bytes accessed | tf_op | source)
XLA Modules:
  0.0 41.7 jit_solution(2408212351371217730)
XLA Ops:
  0.0 40.4 %forget.1 = f32[4,64]{1,0:T(4,128)} custom-call(bf16[1,8192]{1,0:T(2,128)(2,1)} %tokens.1, bf16[1,8192]{1,0:T(2,128)(2,1)} %target.1, bf16[8192,1792]{1,0:T(8,128)(2,1)} %gate.1, bf16[8192,1792]{1,0:T(8,128)(2,1)} %up.1, bf16[1792,8192]{1,0:T(8,128)(2,1)} %down.1, bf16[64,1792]{1,0:T(8,128)(2,1)} %bitcast.5, bf16[64,8192]{1,0:T(8,128)(2,1)} %bitcast.4, ...), custom_call_target="tpu_custom_call" | custom-call | tf_op jit(solution)/shard_map/forget/pallas_call | solution.py:245
  40.4 1.3 %copy.11 = f32[64,4]{0,1:T(4,128)} copy(f32[64,4]{0,1:T(4,128)} %bitcast.6) | data formatting | bytes 2048
